TPU v7x, 256 devices: a whole 4x4x8 slice. The times are simulated.
256 devices in a mesh: band: 32 (over x_hi, z, core), fft: 8 (over x_lo, y).
Axes of the slice: x: 4 (x_hi: 2, x_lo: 2; x = x_hi * 2 + x_lo), y: 4, z: 8, core: 2. Of those that a mesh axis runs over, the one named last changes fastest.
Arguments:
- orbitals: float32 [64, 64, 4096], P('band', 'fft'), may hold values from -5 to 5
Outputs:
- exchange: float32 [64, 64, 4096], P('band', 'fft')
All inputs are finite; a program needn't handle non-finite values.
Results may differ from a plain program's by a relative error of at most 0.00018.
Values sent between devices are 32-bit elements; how exact they have to be, the bound alone decides.
No kernel may reach another device: no remote copies, remote signals or barrier semaphores. Data moves between devices by JAX's collectives and lax.ppermute only.
A program may use at most 64 MiB of HBM per device.

v0:
```python
import math

import jax
import jax.numpy as jnp
from jax import lax
from jax.sharding import PartitionSpec as P

GRID = 64
ROUNDS = 2


EXX_FRACTION = 0.25
SCREEN = 0.05


def broadcast(block, axis, holder):
    block = jnp.where(lax.axis_index(axis) == holder, block, jnp.zeros_like(block))
    return lax.psum(block, axis)


def angle_tables(length):
    indices = jnp.arange(length, dtype=jnp.int32)
    residue = indices[:, None] * indices[None, :] % length
    angles = residue.astype(jnp.float32) * (2.0 * math.pi / length)
    return (jnp.cos(angles), jnp.sin(angles))


def kernel_block(length, y_offset, y_count):
    indices = jnp.arange(length, dtype=jnp.int32)
    signed = jnp.where(indices < length // 2, indices, indices - length).astype(jnp.float32)
    wavenum = signed * (2.0 * math.pi / length)
    y_indices = y_offset + jnp.arange(y_count, dtype=jnp.int32)
    y_signed = jnp.where(y_indices < length // 2, y_indices, y_indices - length).astype(jnp.float32)
    y_wavenum = y_signed * (2.0 * math.pi / length)
    squares = (
        wavenum[:, None, None] ** 2 + y_wavenum[None, :, None] ** 2 + wavenum[None, None, :] ** 2
    )
    guarded = jnp.where(squares > 0, squares, 1.0)
    kernel = jnp.where(
        squares > 0, (1.0 - jnp.exp(-guarded / (4.0 * SCREEN * SCREEN))) / guarded, 0.0
    )
    kernel = kernel / float(length) ** 3
    return jnp.concatenate([kernel, kernel], -1)


def along_axis(spectrum, dimension, cosine_table, sine_table, direction):
    halfway = spectrum.shape[-1] // 2
    if dimension == 1:
        formula = "nakm,ab->nbkm"
    else:
        formula = "nakm,kb->nabm"
    cos_part = jnp.einsum(formula, spectrum, cosine_table, precision=lax.Precision.HIGHEST)
    sin_part = jnp.einsum(formula, spectrum, sine_table, precision=lax.Precision.HIGHEST)
    rotated = jnp.concatenate([-sin_part[..., halfway:], sin_part[..., :halfway]], -1)
    return cos_part + direction * rotated


def forward_yz(density, cosine_table, sine_table):
    z_matrix = jnp.concatenate([cosine_table, -sine_table], 1)
    spectrum = jnp.einsum("nayz,zc->nayc", density, z_matrix, precision=lax.Precision.HIGHEST)
    return along_axis(spectrum, 2, cosine_table, sine_table, -1.0)


def inverse_yz(spectrum, cosine_table, sine_table):
    spectrum = along_axis(spectrum, 2, cosine_table, sine_table, 1.0)
    z_matrix = jnp.concatenate([cosine_table, -sine_table], 0)
    return jnp.einsum("nayc,cz->nayz", spectrum, z_matrix, precision=lax.Precision.HIGHEST)


def per_device(orbitals):
    owned_count, planes, flat_cells = orbitals.shape
    length = GRID
    cosine_table, sine_table = angle_tables(length)
    received = []
    for source_round in range(ROUNDS):
        received.append(broadcast(orbitals, "band", source_round))
    kernel_slab = kernel_block(length, lax.axis_index("fft") * planes, planes)
    accumulated = jnp.zeros((owned_count, planes, flat_cells), jnp.float32)
    for sources in received:
        density = (orbitals[:, None] * sources[None]).reshape(
            owned_count * owned_count, planes, length, length
        )
        spectrum = forward_yz(density, cosine_table, sine_table)
        filtered = (
            along_axis(
                lax.all_to_all(spectrum, "fft", split_axis=2, concat_axis=1, tiled=True),
                1,
                cosine_table,
                sine_table,
                -1.0,
            )
            * kernel_slab
        )
        filtered = along_axis(filtered, 1, cosine_table, sine_table, 1.0)
        returned = lax.all_to_all(filtered, "fft", split_axis=1, concat_axis=2, tiled=True)
        potential = inverse_yz(returned, cosine_table, sine_table)
        potential = potential.reshape(owned_count, owned_count, planes, flat_cells)
        accumulated = accumulated + jnp.sum(potential * sources[None], axis=1)
    return -EXX_FRACTION * accumulated


def solution(mesh):
    return jax.shard_map(
        per_device,
        mesh=mesh,
        in_specs=(P("band", "fft", None),),
        out_specs=P("band", "fft", None),
        check_vma=False,
    )
```

profile of v0, /device:TPU:32, one launch (start us, length us, event | category | flops | bytes accessed | tf_op | source)
XLA Modules:
  0.0 371.7 jit_solution(17171705458724565237)
XLA Ops:
  6.5 0.0 all-reduce.3.cloned.1.call-start
  6.5 1.8 broadcast_select_fusion
  8.3 0.0 all-reduce.3.cloned.1.call-update
  8.3 0.1 fusion.58
  8.5 0.1 fusion.67
  8.7 0.1 broadcast_add_fusion
  8.7 0.2 fusion.29
  8.9 0.0 copy-start
  8.9 0.1 pad_maximum_fusion
  9.1 267.6 %all-reduce.3.cloned.1.call-done = (f32[2,8,4096]{2,1,0:T(8,128)}, f32[2,8,4096]{2,1,0:T(8,128)}) async-done(((f32[2,8,4096]{2,1,0:T(8,128)}, f32[2,8,4096]{2,1,0:T(8,128)}), (f32[2,8,4096]{2,1,0:T(8,128)}, f32[2,8,4096]{2,1,0:T(8,128)})) %all-reduce.3.cloned.1.call-update) | async-done | bytes 524304 | tf_op jit(solution)/shard_map/psum | solution.py:18
  276.6 0.0 copy-done
  276.6 1.1 broadcast_multiply_fusion
  277.8 0.4 mul.281
  278.2 1.0 fusion.77
  279.2 1.2 convolution_bitcast_fusion.14
  280.4 0.4 slice_negate_fusion.7
  280.8 1.4 fusion.9
  282.2 1.6 copy.24
  283.8 4.7 %all-to-all-start = ((f32[4,8,64,128]{3,1,0,2:T(8,128)}), f32[4,8,64,128]{3,1,0,2:T(8,128)S(1)}, u32[]{:S(2)}, u32[]{:S(2)}) async-start(f32[4,8,64,128]{3,1,0,2:T(8,128)} %copy.24), calls=%async_computation | async-start | bytes 2097152 | tf_op jit(solution)/shard_map/all_to_all | solution.py:86
  288.5 0.4 mul.293
  288.9 1.0 fusion.76
  289.9 1.2 convolution_bitcast_fusion.6
  291.1 0.4 slice_negate_fusion.3
  291.5 1.4 fusion.4
  292.9 1.6 copy.36
  294.5 8.7 %all-to-all-done = f32[4,8,64,128]{3,1,0,2:T(8,128)S(1)} async-done(((f32[4,8,64,128]{3,1,0,2:T(8,128)}), f32[4,8,64,128]{3,1,0,2:T(8,128)S(1)}, u32[]{:S(2)}, u32[]{:S(2)}) %all-to-all-start) | async-done | bytes 1048608 | tf_op jit(solution)/shard_map/all_to_all | solution.py:86
  303.2 3.7 %all-to-all-start.2 = ((f32[4,8,64,128]{3,1,0,2:T(8,128)}), f32[4,8,64,128]{3,1,0,2:T(8,128)S(1)}, u32[]{:S(2)}, u32[]{:S(2)}) async-start(f32[4,8,64,128]{3,1,0,2:T(8,128)} %copy.36), calls=%async_computation.2 | async-start | bytes 2097152 | tf_op jit(solution)/shard_map/all_to_all | solution.py:86
  306.9 1.2 convolution_bitcast_fusion.12
  308.1 0.4 slice_negate_fusion.6
  308.5 1.5 fusion.8
  310.0 1.2 convolution_bitcast_fusion.10
  311.1 0.4 slice_negate_fusion.5
  311.5 1.3 fusion.6
  312.9 1.6 copy.30
  314.5 7.3 %all-to-all-done.2 = f32[4,8,64,128]{3,1,0,2:T(8,128)S(1)} async-done(((f32[4,8,64,128]{3,1,0,2:T(8,128)}), f32[4,8,64,128]{3,1,0,2:T(8,128)S(1)}, u32[]{:S(2)}, u32[]{:S(2)}) %all-to-all-start.2) | async-done | bytes 1048608 | tf_op jit(solution)/shard_map/all_to_all | solution.py:86
  321.8 3.6 all-to-all-start.1
  325.5 1.2 convolution_bitcast_fusion.4
  326.6 0.4 slice_negate_fusion.2
  327.0 1.5 fusion.3
  328.5 1.2 convolution_bitcast_fusion.2
  329.6 0.4 slice_negate_fusion.1
  330.0 1.3 fusion.1
  331.4 1.6 copy.42
  333.0 7.5 %all-to-all-done.1 = f32[4,64,8,128]{3,2,0,1:T(8,128)S(1)} async-done(((f32[4,64,8,128]{3,2,0,1:T(8,128)}), f32[4,64,8,128]{3,2,0,1:T(8,128)S(1)}, u32[]{:S(2)}, u32[]{:S(2)}) %all-to-all-start.1) | async-done | bytes 1048608 | tf_op jit(solution)/shard_map/all_to_all | solution.py:95
  340.4 3.8 %all-to-all-start.3 = ((f32[4,64,8,128]{3,2,0,1:T(8,128)}), f32[4,64,8,128]{3,2,0,1:T(8,128)S(1)}, u32[]{:S(2)}, u32[]{:S(2)}) async-start(f32[4,64,8,128]{3,2,0,1:T(8,128)} %copy.42), calls=%async_computation.3 | async-start | bytes 2097152 | tf_op jit(solution)/shard_map/all_to_all | solution.py:95
  344.2 1.2 convolution_bitcast_fusion.8
  345.4 0.4 slice_negate_fusion.4
  345.8 1.4 fusion.5
  347.1 1.0 fusion.34
  348.1 0.4 reshape.85
  348.5 10.6 %all-to-all-done.3 = f32[4,64,8,128]{3,2,0,1:T(8,128)S(1)} async-done(((f32[4,64,8,128]{3,2,0,1:T(8,128)}), f32[4,64,8,128]{3,2,0,1:T(8,128)S(1)}, u32[]{:S(2)}, u32[]{:S(2)}) %all-to-all-start.3) | async-done | bytes 1048608 | tf_op jit(solution)/shard_map/all_to_all | solution.py:95
  359.1 1.2 convolution_bitcast_fusion
  360.2 0.4 slice_negate_fusion
  360.6 1.4 fusion
  362.0 1.0 fusion.33
  363.0 0.0 copy-start.1
  363.0 0.0 copy-start.2
  363.0 0.4 reshape.86
  363.3 0.6 copy-done.1
  363.9 0.1 copy-done.2
  364.0 0.1 multiply_reduce_fusion
  364.1 0.7 add_multiply_fusion
  (2 shorter events, 0.0 us)
Async XLA Ops:
  6.5 270.1 %all-reduce.3.cloned.1.call-start = ((), (), s32[]{:S(2)}) async-start(), calls=%async_computation.4 | async-start | bytes 1048576 | tf_op jit(solution)/shard_map/psum | solution.py:18
  8.9 267.7 %copy-start = (f32[2,8,4096]{2,1,0:T(8,128)S(1)}, f32[2,8,4096]{2,1,0:T(8,128)}, u32[]{:S(2)}) copy-start(f32[2,8,4096]{2,1,0:T(8,128)} %param.1) | copy-start | bytes 786436
  283.8 19.4 %all-to-all-start = ((f32[4,8,64,128]{3,1,0,2:T(8,128)}), f32[4,8,64,128]{3,1,0,2:T(8,128)S(1)}, u32[]{:S(2)}, u32[]{:S(2)}) async-start(f32[4,8,64,128]{3,1,0,2:T(8,128)} %copy.24), calls=%async_computation | async-start | bytes 2097152 | tf_op jit(solution)/shard_map/all_to_all | solution.py:86
  303.2 18.6 %all-to-all-start.2 = ((f32[4,8,64,128]{3,1,0,2:T(8,128)}), f32[4,8,64,128]{3,1,0,2:T(8,128)S(1)}, u32[]{:S(2)}, u32[]{:S(2)}) async-start(f32[4,8,64,128]{3,1,0,2:T(8,128)} %copy.36), calls=%async_computation.2 | async-start | bytes 2097152 | tf_op jit(solution)/shard_map/all_to_all | solution.py:86
  321.8 18.6 %all-to-all-start.1 = ((f32[4,64,8,128]{3,2,0,1:T(8,128)}), f32[4,64,8,128]{3,2,0,1:T(8,128)S(1)}, u32[]{:S(2)}, u32[]{:S(2)}) async-start(f32[4,64,8,128]{3,2,0,1:T(8,128)} %copy.30), calls=%async_computation.1 | async-start | bytes 2097152 | tf_op jit(solution)/shard_map/all_to_all | solution.py:95
  340.4 18.6 %all-to-all-start.3 = ((f32[4,64,8,128]{3,2,0,1:T(8,128)}), f32[4,64,8,128]{3,2,0,1:T(8,128)S(1)}, u32[]{:S(2)}, u32[]{:S(2)}) async-start(f32[4,64,8,128]{3,2,0,1:T(8,128)} %copy.42), calls=%async_computation.3 | async-start | bytes 2097152 | tf_op jit(solution)/shard_map/all_to_all | solution.py:95
  363.0 1.0 copy-start.1
  363.0 1.0 copy-start.2
Sparse Core Ops, SparseCore 0:
  10.0 266.6 all-reduce.2
where the time goes:
time: 378 us; the launch traced here: 372 us
  waiting for transfers between devices  302 us (80%)
  matrix products  24.4 us (6%)
  starting transfers between devices  15.8 us (4%)
  between operations  13.7 us (4%)
  local copies, waits for them, and re-layouts  8.6 us (2%)
  other arithmetic  7.43 us (2%)
    psum x1, waiting for transfers between devices, broadcast(): return lax.psum(block, axis)  268 us
    all_to_all x2, waiting for transfers between devices, per_device(): lax.all_to_all(filtered, 'fft', split_axis=1, concat_axis=2, tiled=True)  18 us
    all_to_all x2, waiting for transfers between devices, per_device(): lax.all_to_all(spectrum, 'fft', split_axis=2, concat_axis=1, tiled=True)  16.1 us
    dot_general x8, matrix products, along_axis(): jnp.einsum(formula, spectrum, cosine_table, precision=lax.Precision.HIGHEST)  11.1 us
    dot_general x8, matrix products, along_axis(): jnp.einsum(formula, spectrum, sine_table, precision=lax.Precision.HIGHEST)  9.25 us
    all_to_all x2, starting transfers between devices, per_device(): lax.all_to_all(spectrum, 'fft', split_axis=2, concat_axis=1, tiled=True)  8.41 us
  transfers between devices with their start and end apart: 5, of which 5 were waited for; matrix products, arithmetic and copies ran while one was open for 7% of the time, Pallas kernels for 0%

commit v1 on v0

v1 whole, which is shorter than its diff:
```python
import math

import jax
import jax.numpy as jnp
from jax import lax
from jax.sharding import PartitionSpec as P

GRID = 64
EXX_FRACTION = 0.25
SCREEN = 0.05
CHIPS = 16


def angle_tables(length):
    indices = jnp.arange(length, dtype=jnp.int32)
    residue = indices[:, None] * indices[None, :] % length
    angles = residue.astype(jnp.float32) * (2.0 * math.pi / length)
    return (jnp.cos(angles), jnp.sin(angles))


def kernel_block(length, y_offset, y_count):
    indices = jnp.arange(length, dtype=jnp.int32)
    signed = jnp.where(indices < length // 2, indices, indices - length).astype(jnp.float32)
    wavenum = signed * (2.0 * math.pi / length)
    y_indices = y_offset + jnp.arange(y_count, dtype=jnp.int32)
    y_signed = jnp.where(y_indices < length // 2, y_indices, y_indices - length).astype(jnp.float32)
    y_wavenum = y_signed * (2.0 * math.pi / length)
    squares = (
        wavenum[:, None, None] ** 2 + y_wavenum[None, :, None] ** 2 + wavenum[None, None, :] ** 2
    )
    guarded = jnp.where(squares > 0, squares, 1.0)
    kernel = jnp.where(
        squares > 0, (1.0 - jnp.exp(-guarded / (4.0 * SCREEN * SCREEN))) / guarded, 0.0
    )
    kernel = kernel / float(length) ** 3
    return jnp.concatenate([kernel, kernel], -1)


def along_axis(spectrum, dimension, cosine_table, sine_table, direction):
    halfway = spectrum.shape[-1] // 2
    if dimension == 1:
        formula = "nakm,ab->nbkm"
    else:
        formula = "nakm,kb->nabm"
    cos_part = jnp.einsum(formula, spectrum, cosine_table, precision=lax.Precision.HIGH)
    sin_part = jnp.einsum(formula, spectrum, sine_table, precision=lax.Precision.HIGH)
    rotated = jnp.concatenate([-sin_part[..., halfway:], sin_part[..., :halfway]], -1)
    return cos_part + direction * rotated


def along_z(fields, cosine_table, sine_table, direction):
    top = jnp.concatenate([cosine_table, direction * sine_table], 1)
    bottom = jnp.concatenate([-direction * sine_table, cosine_table], 1)
    matrix = jnp.concatenate([top, bottom], 0)
    return jnp.einsum("nayz,zc->nayc", fields, matrix, precision=lax.Precision.HIGH)


def fetch_sources(orbitals, same_core):
    pieces = orbitals.reshape(2, 8, 32, 128).transpose(0, 2, 1, 3).reshape(CHIPS, 4, 8, 128)
    spread = lax.all_to_all(pieces, "band", 0, 0, axis_index_groups=same_core, tiled=True)
    mine = jnp.broadcast_to(spread[:1], (CHIPS, 4, 8, 128))
    whole = lax.all_to_all(mine, "band", 0, 0, axis_index_groups=same_core, tiled=True)
    return whole.reshape(2, 32, 8, 128)


def per_device(orbitals):
    owned, planes, flat_cells = orbitals.shape
    length = GRID
    same_core = [[b for b in range(32) if b % 2 == c] for c in (0, 1)]
    first = fetch_sources(orbitals, same_core)
    second = lax.ppermute(first, "band", [(b, b ^ 1) for b in range(32)])
    cosine_table, sine_table = angle_tables(length)
    kernel_slab = kernel_block(length, lax.axis_index("fft") * planes, planes)
    cells = orbitals.reshape(owned, planes, length, length)
    accumulated = jnp.zeros((owned, planes, length, length), jnp.float32)
    for sources in (first, second):
        sources = sources.transpose(0, 2, 1, 3).reshape(2, planes, length, length)
        density = jnp.concatenate([cells * sources[0], cells * sources[1]], -1)
        spectrum = along_z(density, cosine_table, sine_table, -1.0)
        spectrum = along_axis(spectrum, 2, cosine_table, sine_table, -1.0)
        spectrum = lax.all_to_all(spectrum, "fft", split_axis=2, concat_axis=1, tiled=True)
        filtered = along_axis(spectrum, 1, cosine_table, sine_table, -1.0) * kernel_slab
        filtered = along_axis(filtered, 1, cosine_table, sine_table, 1.0)
        returned = lax.all_to_all(filtered, "fft", split_axis=1, concat_axis=2, tiled=True)
        potential = along_axis(returned, 2, cosine_table, sine_table, 1.0)
        potential = along_z(potential, cosine_table, sine_table, 1.0)
        accumulated = accumulated + potential[..., :length] * sources[0]
        accumulated = accumulated + potential[..., length:] * sources[1]
    return (-EXX_FRACTION * accumulated).reshape(owned, planes, flat_cells)


def solution(mesh):
    return jax.shard_map(
        per_device,
        mesh=mesh,
        in_specs=(P("band", "fft", None),),
        out_specs=P("band", "fft", None),
        check_vma=False,
    )
```

time: 378 us -> 102 us (0.27); the launches traced: 372 us -> 102 us
  waiting for transfers between devices: 302 us -> 49.5 us
  starting transfers between devices: 15.8 us -> 30.9 us
  matrix products: 24.4 us -> 11 us
  between operations: 13.7 us -> 0.38 us
  other arithmetic: 7.43 us -> 2.93 us
    psum x1 -> x0, waiting for transfers between devices: 268 us -> none  [broadcast(): return lax.psum(block, axis)]
    all_to_all x0 -> x2, waiting for transfers between devices: none -> 22.2 us  [the longest x1 11.4 us: fetch_sources(): lax.all_to_all(pieces, 'band', 0, 0, axis_index_groups=same_core, tiled=T...]
    all_to_all x0 -> x2, starting transfers between devices: none -> 15.7 us  [the longest x1 11 us: fetch_sources(): lax.all_to_all(pieces, 'band', 0, 0, axis_index_groups=same_core, tiled=T...]
    dot_general x20, matrix products: 24.4 us -> 11 us  [the longest x8 4.82 us: along_axis(): jnp.einsum(formula, spectrum, cosine_table, precision=lax.Precision.HIGH)]
    all_to_all x2, waiting for transfers between devices: 18 us -> 13.1 us  [per_device(): lax.all_to_all(filtered, 'fft', split_axis=1, concat_axis=2, tiled=True)]
  transfers between devices with their start and end apart: 5 -> 7, of which waited for: 5 -> 7; matrix products, arithmetic and copies ran while one was open for 7% -> 12% of each run, Pallas kernels for 0% -> 0%
where the time goes in v1:
time: 102 us
  waiting for transfers between devices  49.5 us (49%)
  starting transfers between devices  30.9 us (30%)
  matrix products  11 us (11%)
  local copies, waits for them, and re-layouts  6.83 us (7%)
  other arithmetic  2.93 us (3%)
    all_to_all x2, waiting for transfers between devices, per_device(): lax.all_to_all(spectrum, 'fft', split_axis=2, concat_axis=1, tiled=True)  13.4 us
    all_to_all x2, waiting for transfers between devices, per_device(): lax.all_to_all(filtered, 'fft', split_axis=1, concat_axis=2, tiled=True)  13.1 us
    all_to_all x1, waiting for transfers between devices, fetch_sources(): lax.all_to_all(pieces, 'band', 0, 0, axis_index_groups=same_core, tiled=T...  11.4 us
    all_to_all x1, starting transfers between devices, fetch_sources(): lax.all_to_all(pieces, 'band', 0, 0, axis_index_groups=same_core, tiled=T...  11 us
    all_to_all x1, waiting for transfers between devices, fetch_sources(): lax.all_to_all(mine, 'band', 0, 0, axis_index_groups=same_core, tiled=True)  10.7 us
    all_to_all x2, starting transfers between devices, per_device(): lax.all_to_all(spectrum, 'fft', split_axis=2, concat_axis=1, tiled=True)  8 us
    all_to_all x2, starting transfers between devices, per_device(): lax.all_to_all(filtered, 'fft', split_axis=1, concat_axis=2, tiled=True)  7.16 us
    dot_general x8, matrix products, along_axis(): jnp.einsum(formula, spectrum, cosine_table, precision=lax.Precision.HIGH)  4.82 us
  transfers between devices with their start and end apart: 7, of which 7 were waited for; matrix products, arithmetic and copies ran while one was open for 12% of the time, Pallas kernels for 0%

profile of v1, /device:TPU:32, one launch (start us, length us, event | category | flops | bytes accessed | tf_op | source)
XLA Modules:
  0.0 101.6 jit_solution(2539866541533684495)
XLA Ops:
  0.0 11.0 %all-to-all-start = ((f32[16,4,8,128]{3,2,1,0:T(8,128)}), f32[16,4,8,128]{3,2,1,0:T(8,128)S(1)}, u32[]{:S(2)}, u32[]{:S(2)}) async-start(f32[16,4,8,128]{3,2,1,0:T(8,128)} %bitcast.183), calls=%async_computation | async-start | bytes 524288 | tf_op jit(solution)/shard_map/all_to_all | solution.py:60
  11.1 11.4 %all-to-all-done = f32[16,4,8,128]{3,2,1,0:T(8,128)S(1)} async-done(((f32[16,4,8,128]{3,2,1,0:T(8,128)}), f32[16,4,8,128]{3,2,1,0:T(8,128)S(1)}, u32[]{:S(2)}, u32[]{:S(2)}) %all-to-all-start) | async-done | bytes 262176 | tf_op jit(solution)/shard_map/all_to_all | solution.py:60
  22.5 0.7 broadcast_in_dim.7
  23.2 4.7 %all-to-all-start.1 = ((f32[16,4,8,128]{3,2,1,0:T(8,128)}), f32[16,4,8,128]{3,2,1,0:T(8,128)S(1)}, u32[]{:S(2)}, u32[]{:S(2)}) async-start(f32[16,4,8,128]{3,2,1,0:T(8,128)} %broadcast_in_dim.7), calls=%async_computation.1 | async-start | bytes 524288 | tf_op jit(solution)/shard_map/all_to_all | solution.py:62
  27.9 0.1 broadcast_add_fusion
  28.0 0.1 broadcast_multiply_fusion.4
  28.1 0.2 fusion.41
  28.3 0.0 copy-start
  28.3 0.1 pad_maximum_fusion
  28.5 10.7 %all-to-all-done.1 = f32[16,4,8,128]{3,2,1,0:T(8,128)S(1)} async-done(((f32[16,4,8,128]{3,2,1,0:T(8,128)}), f32[16,4,8,128]{3,2,1,0:T(8,128)S(1)}, u32[]{:S(2)}, u32[]{:S(2)}) %all-to-all-start.1) | async-done | bytes 262176 | tf_op jit(solution)/shard_map/all_to_all | solution.py:62
  39.2 0.0 collective-permute-start
  39.2 0.1 fusion.78
  39.3 0.0 copy-done
  39.3 0.2 reshape.93
  39.6 0.1 mul.338
  39.8 0.1 mul.341
  39.9 0.8 collective-permute-done
  40.8 0.1 mul.355
  40.9 0.1 mul.358
  41.0 0.2 broadcast_multiply_fusion.3
  41.3 0.5 fusion.18
  41.7 0.5 convolution_bitcast_fusion.6
  42.3 0.5 fusion.14
  42.8 0.5 convolution_bitcast_fusion.14
  43.3 0.2 slice_negate_fusion.7
  43.6 0.6 fusion
  44.2 1.1 %copy.66 = f32[2,8,64,128]{3,1,0,2:T(8,128)} copy(f32[2,8,64,128]{3,2,1,0:T(8,128)S(1)} %fusion) | data formatting | bytes 1048576 | tf_op jit(solution)/shard_map/add | solution.py:48
  45.3 4.5 %all-to-all-start.2 = ((f32[2,8,64,128]{3,1,0,2:T(8,128)}), f32[2,8,64,128]{3,1,0,2:T(8,128)S(1)}, u32[]{:S(2)}, u32[]{:S(2)}) async-start(f32[2,8,64,128]{3,1,0,2:T(8,128)} %copy.66), calls=%async_computation.2 | async-start | bytes 1048576 | tf_op jit(solution)/shard_map/all_to_all | solution.py:81
  49.8 0.2 slice_negate_fusion.3
  50.0 0.6 fusion.5
  50.6 1.1 %copy.80 = f32[2,8,64,128]{3,1,0,2:T(8,128)} copy(f32[2,8,64,128]{3,2,1,0:T(8,128)S(1)} %fusion.5) | data formatting | bytes 1048576 | tf_op jit(solution)/shard_map/add | solution.py:48
  51.7 7.8 %all-to-all-done.2 = f32[2,8,64,128]{3,1,0,2:T(8,128)S(1)} async-done(((f32[2,8,64,128]{3,1,0,2:T(8,128)}), f32[2,8,64,128]{3,1,0,2:T(8,128)S(1)}, u32[]{:S(2)}, u32[]{:S(2)}) %all-to-all-start.2) | async-done | bytes 524320 | tf_op jit(solution)/shard_map/all_to_all | solution.py:81
  59.5 3.5 %all-to-all-start.4 = ((f32[2,8,64,128]{3,1,0,2:T(8,128)}), f32[2,8,64,128]{3,1,0,2:T(8,128)S(1)}, u32[]{:S(2)}, u32[]{:S(2)}) async-start(f32[2,8,64,128]{3,1,0,2:T(8,128)} %copy.80), calls=%async_computation.4 | async-start | bytes 1048576 | tf_op jit(solution)/shard_map/all_to_all | solution.py:81
  63.0 0.6 convolution_bitcast_fusion.12
  63.6 0.2 slice_negate_fusion.6
  63.8 0.6 fusion.2
  64.4 0.6 convolution_bitcast_fusion.10
  64.9 0.2 slice_negate_fusion.5
  65.2 0.6 fusion.3
  65.8 1.1 %copy.72 = f32[2,64,8,128]{3,2,0,1:T(8,128)} copy(f32[2,64,8,128]{3,1,2,0:T(8,128)S(1)} %fusion.3) | data formatting | bytes 1048576 | tf_op jit(solution)/shard_map/add | solution.py:48
  66.9 5.6 %all-to-all-done.4 = f32[2,8,64,128]{3,1,0,2:T(8,128)S(1)} async-done(((f32[2,8,64,128]{3,1,0,2:T(8,128)}), f32[2,8,64,128]{3,1,0,2:T(8,128)S(1)}, u32[]{:S(2)}, u32[]{:S(2)}) %all-to-all-start.4) | async-done | bytes 524320 | tf_op jit(solution)/shard_map/all_to_all | solution.py:81
  72.5 3.7 %all-to-all-start.3 = ((f32[2,64,8,128]{3,2,0,1:T(8,128)}), f32[2,64,8,128]{3,2,0,1:T(8,128)S(1)}, u32[]{:S(2)}, u32[]{:S(2)}) async-start(f32[2,64,8,128]{3,2,0,1:T(8,128)} %copy.72), calls=%async_computation.3 | async-start | bytes 1048576 | tf_op jit(solution)/shard_map/all_to_all | solution.py:84
  76.2 0.5 convolution_bitcast_fusion.4
  76.7 0.2 slice_negate_fusion.2
  77.0 0.6 fusion.7
  77.6 0.6 convolution_bitcast_fusion.2
  78.1 0.2 slice_negate_fusion.1
  78.3 0.6 fusion.8
  78.9 1.1 %copy.86 = f32[2,64,8,128]{3,2,0,1:T(8,128)} copy(f32[2,64,8,128]{3,1,2,0:T(8,128)S(1)} %fusion.8) | data formatting | bytes 1048576 | tf_op jit(solution)/shard_map/add | solution.py:48
  80.0 5.5 %all-to-all-done.3 = f32[2,64,8,128]{3,2,0,1:T(8,128)S(1)} async-done(((f32[2,64,8,128]{3,2,0,1:T(8,128)}), f32[2,64,8,128]{3,2,0,1:T(8,128)S(1)}, u32[]{:S(2)}, u32[]{:S(2)}) %all-to-all-start.3) | async-done | bytes 524320 | tf_op jit(solution)/shard_map/all_to_all | solution.py:84
  85.5 3.5 %all-to-all-start.5 = ((f32[2,64,8,128]{3,2,0,1:T(8,128)}), f32[2,64,8,128]{3,2,0,1:T(8,128)S(1)}, u32[]{:S(2)}, u32[]{:S(2)}) async-start(f32[2,64,8,128]{3,2,0,1:T(8,128)} %copy.86), calls=%async_computation.5 | async-start | bytes 1048576 | tf_op jit(solution)/shard_map/all_to_all | solution.py:84
  89.0 0.5 convolution_bitcast_fusion.8
  89.6 0.2 slice_negate_fusion.4
  89.8 0.6 fusion.4
  90.4 0.4 fusion.51
  90.8 7.7 %all-to-all-done.5 = f32[2,64,8,128]{3,2,0,1:T(8,128)S(1)} async-done(((f32[2,64,8,128]{3,2,0,1:T(8,128)}), f32[2,64,8,128]{3,2,0,1:T(8,128)S(1)}, u32[]{:S(2)}, u32[]{:S(2)}) %all-to-all-start.5) | async-done | bytes 524320 | tf_op jit(solution)/shard_map/all_to_all | solution.py:84
  98.5 0.5 convolution_bitcast_fusion
  99.1 0.2 slice_negate_fusion
  99.3 0.6 fusion.9
  99.9 0.4 fusion.49
  100.3 0.4 fusion.11
  100.7 0.9 reshape.97
  (9 shorter events, 0.2 us)
Async XLA Ops:
  0.0 22.5 %all-to-all-start = ((f32[16,4,8,128]{3,2,1,0:T(8,128)}), f32[16,4,8,128]{3,2,1,0:T(8,128)S(1)}, u32[]{:S(2)}, u32[]{:S(2)}) async-start(f32[16,4,8,128]{3,2,1,0:T(8,128)} %bitcast.183), calls=%async_computation | async-start | bytes 524288 | tf_op jit(solution)/shard_map/all_to_all | solution.py:60
  23.2 15.9 %all-to-all-start.1 = ((f32[16,4,8,128]{3,2,1,0:T(8,128)}), f32[16,4,8,128]{3,2,1,0:T(8,128)S(1)}, u32[]{:S(2)}, u32[]{:S(2)}) async-start(f32[16,4,8,128]{3,2,1,0:T(8,128)} %broadcast_in_dim.7), calls=%async_computation.1 | async-start | bytes 524288 | tf_op jit(solution)/shard_map/all_to_all | solution.py:62
  28.3 11.0 %copy-start = (f32[2,8,4096]{2,1,0:T(8,128)S(1)}, f32[2,8,4096]{2,1,0:T(8,128)}, u32[]{:S(2)}) copy-start(f32[2,8,4096]{2,1,0:T(8,128)} %param.1) | copy-start | bytes 786436
  39.2 1.5 %collective-permute-start = (f32[2,32,8,128]{3,2,1,0:T(8,128)S(1)}, f32[2,32,8,128]{3,2,1,0:T(8,128)S(1)}, u32[]{:S(2)}, u32[]{:S(2)}) collective-permute-start(f32[2,32,8,128]{3,2,1,0:T(8,128)S(1)} %bitcast.184), channel_id=1, source_target_pairs={{0,8},{8,0},{16,24},{24,16},{32,40},{40,32},{48,56},{56,48},{64,72... | collective-permute-start | bytes 786440 | tf_op jit(solution)/shard_map/ppermute | solution.py:71
  45.3 14.2 %all-to-all-start.2 = ((f32[2,8,64,128]{3,1,0,2:T(8,128)}), f32[2,8,64,128]{3,1,0,2:T(8,128)S(1)}, u32[]{:S(2)}, u32[]{:S(2)}) async-start(f32[2,8,64,128]{3,1,0,2:T(8,128)} %copy.66), calls=%async_computation.2 | async-start | bytes 1048576 | tf_op jit(solution)/shard_map/all_to_all | solution.py:81
  59.5 13.0 %all-to-all-start.4 = ((f32[2,8,64,128]{3,1,0,2:T(8,128)}), f32[2,8,64,128]{3,1,0,2:T(8,128)S(1)}, u32[]{:S(2)}, u32[]{:S(2)}) async-start(f32[2,8,64,128]{3,1,0,2:T(8,128)} %copy.80), calls=%async_computation.4 | async-start | bytes 1048576 | tf_op jit(solution)/shard_map/all_to_all | solution.py:81
  72.5 13.0 %all-to-all-start.3 = ((f32[2,64,8,128]{3,2,0,1:T(8,128)}), f32[2,64,8,128]{3,2,0,1:T(8,128)S(1)}, u32[]{:S(2)}, u32[]{:S(2)}) async-start(f32[2,64,8,128]{3,2,0,1:T(8,128)} %copy.72), calls=%async_computation.3 | async-start | bytes 1048576 | tf_op jit(solution)/shard_map/all_to_all | solution.py:84
  85.5 13.0 %all-to-all-start.5 = ((f32[2,64,8,128]{3,2,0,1:T(8,128)}), f32[2,64,8,128]{3,2,0,1:T(8,128)S(1)}, u32[]{:S(2)}, u32[]{:S(2)}) async-start(f32[2,64,8,128]{3,2,0,1:T(8,128)} %copy.86), calls=%async_computation.5 | async-start | bytes 1048576 | tf_op jit(solution)/shard_map/all_to_all | solution.py:84

commit v2 on v1

v2 whole, which is shorter than its diff:
```python
import functools
import math

import jax
import jax.numpy as jnp
import numpy as np
from jax import lax
from jax.experimental import pallas as pl
from jax.experimental.pallas import tpu as pltpu
from jax.sharding import PartitionSpec as P

GRID = 64
EXX_FRACTION = 0.25
SCREEN = 0.05
CHIPS = 16
PLANES = 8
LANES = 128


def split_table(table):
    high = np.asarray(table, np.float32).astype(jnp.bfloat16)
    low = (table - high.astype(np.float64)).astype(np.float32).astype(jnp.bfloat16)
    return high, low


def left_table(direction):
    index = np.arange(GRID)
    angles = (index[:, None] * index[None, :] % GRID) * (2.0 * math.pi / GRID)
    cosine, sine = np.cos(angles), direction * np.sin(angles)
    high, low = split_table(np.block([[cosine, -sine], [sine, cosine]]))
    return np.concatenate([high, high, low], 1)


def right_table(direction):
    index = np.arange(GRID)
    angles = (index[:, None] * index[None, :] % GRID) * (2.0 * math.pi / GRID)
    cosine, sine = np.cos(angles), direction * np.sin(angles)
    pair = np.eye(2)
    table = np.block(
        [
            [np.kron(pair, cosine), np.kron(pair, sine)],
            [np.kron(pair, -sine), np.kron(pair, cosine)],
        ]
    )
    high, low = split_table(table)
    return np.concatenate([high, high, low], 0)


def filter_table(y_offset):
    indices = jnp.arange(GRID, dtype=jnp.int32)
    signed = jnp.where(indices < GRID // 2, indices, indices - GRID).astype(jnp.float32)
    wavenum = signed * (2.0 * math.pi / GRID)
    y_indices = y_offset + jnp.arange(PLANES, dtype=jnp.int32)
    y_signed = jnp.where(y_indices < GRID // 2, y_indices, y_indices - GRID).astype(jnp.float32)
    y_wavenum = y_signed * (2.0 * math.pi / GRID)
    wide = jnp.concatenate([wavenum, wavenum])
    squares = wavenum[None, :, None] ** 2 + y_wavenum[:, None, None] ** 2 + wide[None, None, :] ** 2
    guarded = jnp.where(squares > 0, squares, 1.0)
    kernel = jnp.where(
        squares > 0, (1.0 - jnp.exp(-guarded / (4.0 * SCREEN * SCREEN))) / guarded, 0.0
    )
    return kernel * (-EXX_FRACTION / float(GRID) ** 3)


def parts(values):
    high = values.astype(jnp.bfloat16)
    low = (values - high.astype(jnp.float32)).astype(jnp.bfloat16)
    return high, low


def times_left(table, values):
    high, low = parts(values)
    stacked = jnp.concatenate([high, low, high], 0)
    return jnp.dot(table, stacked, preferred_element_type=jnp.float32)


def times_right(values, table):
    high, low = parts(values)
    stacked = jnp.concatenate([high, low, high], 1)
    return jnp.dot(stacked, table, preferred_element_type=jnp.float32)


def pair_sources(own_ref, other_ref, part, y_half, low_lanes):
    own, other = own_ref[part, y_half], other_ref[part, y_half]
    even = jnp.where(low_lanes, own, pltpu.roll(other, GRID, 1))
    odd = jnp.where(low_lanes, pltpu.roll(own, GRID, 1), other)
    return even, odd


def forward_kernel(orb_ref, own_ref, other_ref, right_ref, left_ref, out_ref, pair_ref, work_ref):
    low_lanes = lax.broadcasted_iota(jnp.int32, (PLANES, LANES), 1) < GRID
    for y_half in range(GRID // 2):
        for part in range(2):
            even, odd = pair_sources(own_ref, other_ref, part, y_half, low_lanes)
            for i in range(2):
                tile = orb_ref[i, :, y_half * LANES : (y_half + 1) * LANES]
                turned = pltpu.roll(tile, GRID, 1)
                base = y_half * 2 * PLANES
                lanes = slice(part * LANES, (part + 1) * LANES)
                pair_ref[i, base : base + PLANES, lanes] = (
                    jnp.where(low_lanes, tile, turned) * even
                )
                pair_ref[i, base + PLANES : base + 2 * PLANES, lanes] = (
                    jnp.where(low_lanes, turned, tile) * odd
                )
    for i in range(2):
        result = times_right(pair_ref[i], right_ref[...])
        work_ref[0] = result[:, :LANES]
        work_ref[1] = result[:, LANES:]
        for x in range(0, PLANES, 2):
            columns = []
            for plane in (x, x + 1):
                rows = [work_ref[part, pl.ds(plane, GRID, stride=PLANES), :] for part in range(2)]
                columns.append(jnp.concatenate(rows, 0))
            result = times_left(left_ref[...], jnp.concatenate(columns, 1))
            for k in range(2):
                for part in range(2):
                    block = result[part * GRID : (part + 1) * GRID, k * LANES : (k + 1) * LANES]
                    out_ref[:, i, x + k, part] = block.reshape(8, PLANES, LANES)


def middle_kernel(in_ref, forth_ref, back_ref, filter_ref, out_ref):
    for i in range(2):
        for ky in range(0, PLANES, 2):
            columns = []
            for y in (ky, ky + 1):
                rows = []
                for part in range(2):
                    for block in range(8):
                        start = block * 256 + i * 128 + part * 8 + y
                        rows.append(in_ref[pl.ds(start, PLANES, stride=16), :])
                columns.append(jnp.concatenate(rows, 0))
            spectrum = times_left(forth_ref[...], jnp.concatenate(columns, 1))
            scale = jnp.concatenate([filter_ref[ky], filter_ref[ky + 1]], 1)
            spectrum = spectrum * jnp.concatenate([scale, scale], 0)
            result = times_left(back_ref[...], spectrum)
            for k in range(2):
                for part in range(2):
                    for block in range(8):
                        start = block * 256 + i * 128 + part * 8 + ky + k
                        top = part * GRID + block * PLANES
                        out_ref[pl.ds(start, PLANES, stride=16), :] = result[
                            top : top + PLANES, k * LANES : (k + 1) * LANES
                        ]


def inverse_kernel(in_ref, own_ref, other_ref, right_ref, left_ref, out_ref, work_ref):
    low_lanes = lax.broadcasted_iota(jnp.int32, (PLANES, LANES), 1) < GRID
    for i in range(2):
        for x in range(0, PLANES, 2):
            columns = []
            for plane in (x, x + 1):
                rows = [in_ref[:, i, plane, part].reshape(GRID, LANES) for part in range(2)]
                columns.append(jnp.concatenate(rows, 0))
            result = times_left(left_ref[...], jnp.concatenate(columns, 1))
            for k in range(2):
                for part in range(2):
                    work_ref[part, pl.ds(x + k, GRID, stride=PLANES), :] = result[
                        part * GRID : (part + 1) * GRID, k * LANES : (k + 1) * LANES
                    ]
        potential = times_right(jnp.concatenate([work_ref[0], work_ref[1]], 1), right_ref[...])
        for y_half in range(GRID // 2):
            sums = [0.0, 0.0]
            for part in range(2):
                pair = pair_sources(own_ref, other_ref, part, y_half, low_lanes)
                for odd in range(2):
                    base = (y_half * 2 + odd) * PLANES
                    values = potential[base : base + PLANES, part * LANES : (part + 1) * LANES]
                    sums[odd] = sums[odd] + values * pair[odd]
            even, odd = (s + pltpu.roll(s, GRID, 1) for s in sums)
            out_ref[i, :, y_half * LANES : (y_half + 1) * LANES] = jnp.where(low_lanes, even, odd)


def local_call(kernel, shape, scratch):
    return pl.pallas_call(
        kernel,
        out_shape=jax.ShapeDtypeStruct(shape, jnp.float32),
        scratch_shapes=scratch,
        compiler_params=pltpu.CompilerParams(vmem_limit_bytes=24 << 20),
    )


def fetch_sources(orbitals, same_core):
    pieces = orbitals.reshape(2, 8, 32, 128).transpose(0, 2, 1, 3).reshape(CHIPS, 4, 8, 128)
    spread = lax.all_to_all(pieces, "band", 0, 0, axis_index_groups=same_core, tiled=True)
    mine = jnp.broadcast_to(spread[:1], (CHIPS, 4, 8, 128))
    whole = lax.all_to_all(mine, "band", 0, 0, axis_index_groups=same_core, tiled=True)
    return whole.reshape(2, 32, 8, 128)


def per_device(orbitals):
    same_core = [[b for b in range(32) if b % 2 == c] for c in (0, 1)]
    own = fetch_sources(orbitals, same_core)
    other = lax.ppermute(own, "band", [(b, b ^ 1) for b in range(32)])
    filters = filter_table(lax.axis_index("fft") * PLANES)
    left_forth, left_back = (jnp.asarray(left_table(s)) for s in (-1.0, 1.0))
    right_forth, right_back = (jnp.asarray(right_table(s)) for s in (-1.0, 1.0))
    rows = PLANES * GRID
    work = pltpu.VMEM((2, rows, LANES), jnp.float32)
    spectrum = local_call(
        forward_kernel,
        (8, 2, PLANES, 2, PLANES, LANES),
        [pltpu.VMEM((2, rows, 2 * LANES), jnp.float32), work],
    )(orbitals, own, other, right_forth, left_forth)
    spectrum = lax.all_to_all(spectrum, "fft", 0, 0, tiled=True)
    filtered = local_call(middle_kernel, (2048, LANES), [])(
        spectrum.reshape(2048, LANES), left_forth, left_back, filters
    )
    filtered = filtered.reshape(8, 2, PLANES, 2, PLANES, LANES)
    returned = lax.all_to_all(filtered, "fft", 0, 0, tiled=True)
    return local_call(inverse_kernel, (2, PLANES, GRID * GRID), [work])(
        returned, own, other, right_back, left_back
    )


def solution(mesh):
    return jax.shard_map(
        per_device,
        mesh=mesh,
        in_specs=(P("band", "fft", None),),
        out_specs=P("band", "fft", None),
        check_vma=False,
    )
```

time: 102 us -> 85.2 us (0.84)
  blocking collectives: 0 us -> 57.9 us
  waiting for transfers between devices: 49.5 us -> 16.3 us
  starting transfers between devices: 30.9 us -> 4.5 us
  matrix products: 11 us -> 0 us
  local copies, waits for them, and re-layouts: 6.83 us -> 0.05 us
  Pallas kernels: 0 us -> 5.74 us
  other arithmetic: 2.93 us -> 0.34 us
    all_to_all x0 -> x3, blocking collectives: none -> 57.9 us  [the longest x1 22.5 us: fetch_sources(): lax.all_to_all(pieces, 'band', 0, 0, axis_index_groups=same_core, tiled=T...]
    all_to_all x6 -> x1, waiting for transfers between devices: 48.7 us -> 14.7 us  [per_device(): spectrum = lax.all_to_all(spectrum, 'fft', 0, 0, tiled=True)]
    all_to_all x6 -> x1, starting transfers between devices: 30.9 us -> 4.5 us  [per_device(): spectrum = lax.all_to_all(spectrum, 'fft', 0, 0, tiled=True)]
    dot_general x20 -> x0, matrix products: 11 us -> none  [the longest x8 4.82 us: along_axis(): jnp.einsum(formula, spectrum, cosine_table, precision=lax.Precision.HIGH)]
    pallas_call x0 -> x3, Pallas kernels: none -> 5.74 us  [the longest x1 2.89 us: per_device(): local_call(forward_kernel, (8, 2, PLANES, 2, PLANES, LANES), [pltpu.VMEM(...]
    add x4 -> x0, local copies, waits for them, and re-layouts: 4.44 us -> none  [along_axis(): return cos_part + direction * rotated]
    neg x8 -> x0, other arithmetic: 1.66 us -> none  [along_axis(): -sin_part[..., halfway:]]
    reshape x2 -> x0, local copies, waits for them, and re-layouts: 1.1 us -> none  [the longest x1 0.89 us: per_device(): return (-EXX_FRACTION * accumulated).reshape(owned, planes, flat_cells)]
  transfers between devices with their start and end apart: 7 -> 2, of which waited for: 7 -> 2; matrix products, arithmetic and copies ran while one was open for 12% -> 0% of each run, Pallas kernels for 0% -> 0%
where the time goes in v2:
time: 85.2 us; the launch traced here: 84.9 us
  blocking collectives  57.9 us (68%)
  waiting for transfers between devices  16.3 us (19%)
  Pallas kernels  5.74 us (7%)
  starting transfers between devices  4.5 us (5%)
    all_to_all x1, blocking collectives, fetch_sources(): lax.all_to_all(pieces, 'band', 0, 0, axis_index_groups=same_core, tiled=T...  22.5 us
    all_to_all x1, blocking collectives, per_device(): returned = lax.all_to_all(filtered, 'fft', 0, 0, tiled=True)  19.5 us
    all_to_all x1, blocking collectives, fetch_sources(): lax.all_to_all(mine, 'band', 0, 0, axis_index_groups=same_core, tiled=True)  15.9 us
    all_to_all x1, waiting for transfers between devices, per_device(): spectrum = lax.all_to_all(spectrum, 'fft', 0, 0, tiled=True)  14.7 us
    all_to_all x1, starting transfers between devices, per_device(): spectrum = lax.all_to_all(spectrum, 'fft', 0, 0, tiled=True)  4.5 us
    pallas_call x1, Pallas kernels, per_device(): local_call(forward_kernel, (8, 2, PLANES, 2, PLANES, LANES), [pltpu.VMEM(...  2.89 us
    pallas_call x1, Pallas kernels, per_device(): local_call(inverse_kernel, (2, PLANES, GRID * GRID), [work])  1.77 us
  transfers between devices with their start and end apart: 2, of which 2 were waited for; matrix products, arithmetic and copies ran while one was open for 0% of the time, Pallas kernels for 0%

profile of v2, /device:TPU:32, one launch (start us, length us, event | category | flops | bytes accessed | tf_op | source)
XLA Modules:
  0.0 84.9 jit_solution(17695459820755061551)
XLA Ops:
  0.0 22.5 %all_to_all.20 = f32[16,4,8,128]{3,2,1,0:T(8,128)S(1)} all-to-all(f32[16,4,8,128]{3,2,1,0:T(8,128)} %bitcast.15), channel_id=1, replica_groups={{0,16,32,48,64,80,96,112,128,144,160,176,192,208,224,240},{8,24,40,56,7..., dimensions={0} | all-to-all | bytes 524288 | tf_op jit(solution)/shard_map/all_to_all | solution.py:185
  22.5 0.0 copy-start.4
  22.5 0.0 copy-start
  22.5 0.0 copy-start.2
  22.6 15.9 %all_to_all.21 = f32[16,4,8,128]{3,2,1,0:T(8,128)S(1)} all-to-all(f32[16,4,8,128]{3,2,1,0:T(8,128)S(1)} %broadcast_in_dim.14), channel_id=1, replica_groups={{0,16,32,48,64,80,96,112,128,144,160,176,192,208,224,240},{8,24,40,56,7..., dimensions={0} | all-to-all | bytes 524288 | tf_op jit(solution)/shard_map/all_to_all | solution.py:187
  38.4 0.0 collective-permute-start
  38.4 1.5 %collective-permute-done.other_ref = f32[2,32,8,128]{3,2,1,0:T(8,128)S(1)} collective-permute-done((f32[2,32,8,128]{3,2,1,0:T(8,128)S(1)}, f32[2,32,8,128]{3,2,1,0:T(8,128)S(1)}, u32[]{:S(2)}, u32[]{:S(2)}) %collective-permute-start) | collective-permute-done | bytes 262176 | tf_op jit(solution)/shard_map/ppermute | solution.py:194
  40.0 0.0 copy-done.4
  40.0 0.0 copy-done
  40.0 0.0 copy-done.2
  40.0 2.9 %shard_map.55 = f32[8,2,8,2,8,128]{5,4,3,2,1,0:T(8,128)} custom-call(f32[2,8,4096]{2,1,0:T(8,128)S(1)} %copy-done, f32[2,32,8,128]{3,2,1,0:T(8,128)S(1)} %bitcast.13, f32[2,32,8,128]{3,2,1,0:T(8,128)S(1)} %collective-permute-done.other_ref, bf16[768,256]{1,0:T(8,128)(2,1)S(1)} %copy-done.4, bf16[128,384]{1,0:T(8,128)(2,1)S(1)} %copy-done.2), custom_call_target="tpu_custom_call" | custom-call | tf_op jit(solution)/shard_map/pallas_call | solution.py:200
  42.9 4.5 %all-to-all-start.2 = ((f32[8,2,8,2,8,128]{5,4,3,2,1,0:T(8,128)}), f32[8,2,8,2,8,128]{5,4,3,2,1,0:T(8,128)S(1)}, u32[]{:S(2)}, u32[]{:S(2)}) async-start(f32[8,2,8,2,8,128]{5,4,3,2,1,0:T(8,128)} %shard_map.55), calls=%async_computation.2 | async-start | bytes 2097152 | tf_op jit(solution)/shard_map/all_to_all | solution.py:205
  47.4 0.1 maximum_multiply_fusion
  47.5 0.1 broadcast_add_fusion
  47.5 0.0 copy-start.1
  47.6 0.2 fusion.3.filter_ref
  47.7 14.7 %all-to-all-done.2 = f32[8,2,8,2,8,128]{5,4,3,2,1,0:T(8,128)S(1)} async-done(((f32[8,2,8,2,8,128]{5,4,3,2,1,0:T(8,128)}), f32[8,2,8,2,8,128]{5,4,3,2,1,0:T(8,128)S(1)}, u32[]{:S(2)}, u32[]{:S(2)}) %all-to-all-start.2) | async-done | bytes 1048608 | tf_op jit(solution)/shard_map/all_to_all | solution.py:205
  62.5 0.0 copy-done.1
  62.5 1.1 %shard_map.56 = f32[2048,128]{1,0:T(8,128)S(1)} custom-call(f32[2048,128]{1,0:T(8,128)S(1)} %bitcast.10, bf16[128,384]{1,0:T(8,128)(2,1)S(1)} %copy-done.2, bf16[128,384]{1,0:T(8,128)(2,1)S(1)} %copy-done.1, f32[8,64,128]{2,1,0:T(8,128)S(1)} %fusion.3.filter_ref), custom_call_target="tpu_custom_call" | custom-call | tf_op jit(solution)/shard_map/pallas_call | solution.py:206
  63.6 0.0 copy-start.3
  63.6 19.5 %all_to_all.22.in_ref = f32[8,2,8,2,8,128]{5,4,3,2,1,0:T(8,128)S(1)} all-to-all(f32[8,2,8,2,8,128]{5,4,3,2,1,0:T(8,128)S(1)} %bitcast.11), channel_id=1, replica_groups=mesh['band'=32,'fft'=8] {'fft'}, dimensions={0} | all-to-all | bytes 2097152 | tf_op jit(solution)/shard_map/all_to_all | solution.py:210
  83.1 0.0 copy-done.3
  83.1 1.8 %shard_map.57 = f32[2,8,4096]{2,1,0:T(8,128)} custom-call(f32[8,2,8,2,8,128]{5,4,3,2,1,0:T(8,128)S(1)} %all_to_all.22.in_ref, f32[2,32,8,128]{3,2,1,0:T(8,128)S(1)} %bitcast.14, f32[2,32,8,128]{3,2,1,0:T(8,128)S(1)} %collective-permute-done.other_ref, bf16[768,256]{1,0:T(8,128)(2,1)S(1)} %copy-done.3, bf16[128,384]{1,0:T(8,128)(2,1)S(1)} %copy-done.1), custom_call_target="tpu_custom_call" | custom-call | tf_op jit(solution)/shard_map/pallas_call | solution.py:211
  (5 shorter events, 0.0 us)
Async XLA Ops:
  22.5 17.5 %copy-start.4 = (bf16[768,256]{1,0:T(8,128)(2,1)S(1)}, bf16[768,256]{1,0:T(8,128)(2,1)}, u32[]{:S(2)}) copy-start(bf16[768,256]{1,0:T(8,128)(2,1)} %constant.38.clone.right_ref) | copy-start | bytes 1179652
  22.5 17.4 %copy-start = (f32[2,8,4096]{2,1,0:T(8,128)S(1)}, f32[2,8,4096]{2,1,0:T(8,128)}, u32[]{:S(2)}) copy-start(f32[2,8,4096]{2,1,0:T(8,128)} %orb_ref.1) | copy-start | bytes 786436
  22.5 17.4 %copy-start.2 = (bf16[128,384]{1,0:T(8,128)(2,1)S(1)}, bf16[128,384]{1,0:T(8,128)(2,1)}, u32[]{:S(2)}) copy-start(bf16[128,384]{1,0:T(8,128)(2,1)} %constant.11.clone.left_ref.forth_ref) | copy-start | bytes 294916
  38.4 1.5 %collective-permute-start = (f32[2,32,8,128]{3,2,1,0:T(8,128)S(1)}, f32[2,32,8,128]{3,2,1,0:T(8,128)S(1)}, u32[]{:S(2)}, u32[]{:S(2)}) collective-permute-start(f32[2,32,8,128]{3,2,1,0:T(8,128)S(1)} %bitcast.12), channel_id=1, source_target_pairs={{0,8},{8,0},{16,24},{24,16},{32,40},{40,32},{48,56},{56,48},{64,72... | collective-permute-start | bytes 786440 | tf_op jit(solution)/shard_map/ppermute | solution.py:194
  42.9 19.6 %all-to-all-start.2 = ((f32[8,2,8,2,8,128]{5,4,3,2,1,0:T(8,128)}), f32[8,2,8,2,8,128]{5,4,3,2,1,0:T(8,128)S(1)}, u32[]{:S(2)}, u32[]{:S(2)}) async-start(f32[8,2,8,2,8,128]{5,4,3,2,1,0:T(8,128)} %shard_map.55), calls=%async_computation.2 | async-start | bytes 2097152 | tf_op jit(solution)/shard_map/all_to_all | solution.py:205
  47.5 14.9 %copy-start.1 = (bf16[128,384]{1,0:T(8,128)(2,1)S(1)}, bf16[128,384]{1,0:T(8,128)(2,1)}, u32[]{:S(2)}) copy-start(bf16[128,384]{1,0:T(8,128)(2,1)} %constant.12.clone.back_ref.left_ref) | copy-start | bytes 294916
  63.6 19.5 %copy-start.3 = (bf16[768,256]{1,0:T(8,128)(2,1)S(1)}, bf16[768,256]{1,0:T(8,128)(2,1)}, u32[]{:S(2)}) copy-start(bf16[768,256]{1,0:T(8,128)(2,1)} %constant.39.clone.right_ref) | copy-start | bytes 1179652
